TPU v7x, 32 devices: a whole 2x2x4 slice. The times are simulated.
32 devices in a mesh: row: 4 (over y, core), col: 8 (over z, x).
Axes of the slice: x: 2, y: 2, z: 4, core: 2. Of those that a mesh axis runs over, the one named last changes fastest.
Arguments:
- outside: bfloat16 [2048, 4096], P('row', 'col'), may hold values from 0.0099 to 17.5
- inside_head: bfloat16 [2048, 4096], P('row', 'col'), may hold values from 0.0099 to 17.5
- inside_tail: bfloat16 [2048, 4096], P('row', 'col'), may hold values from 0.0099 to 17.5
- inside_pair: float32 [512, 4096], P(None, 'col'), may hold values from 0.4 to 1.6
- seq_head: int32 [1, 4096], P(None, 'col'), may hold values from 0 to 3
- seq_tail: int32 [1, 4096], P(None, 'col'), may hold values from 0 to 3
- pair_mask: int32 [4, 32], P(None, 'col'), may hold values 0 or 1
- split_weight: float32 [4], replicated, may hold values from 0.5 to 2
- pair_weight: float32 [4, 4], replicated, may hold values from 0.5 to 2
- span_blocks: int32 [1], replicated, may hold values from 8 to 63
- partition: float32 [1], replicated, may hold values from 1 to 3
Outputs:
- outside_out: float32 [2048, 4096], P('row', 'col')
- prob_out: float32 [2048, 4096], P('row', 'col')
All inputs are finite; a program needn't handle non-finite values. No bound on the sum of `pair_mask` on one device may be relied on, other than what follows from the above.
Results may differ from a plain program's by a relative error of at most 0.0003.
Values may be sent and summed in bfloat16 or wider, within the bound.
No kernel may reach another device: no remote copies, remote signals or barrier semaphores. Data moves between devices by JAX's collectives and lax.ppermute only.
A program may use at most 64 MiB of HBM per device.

v0:
```python
import jax
import jax.numpy as jnp
from jax import lax
from jax.sharding import PartitionSpec as P

precise = lax.Precision.HIGHEST


def passed_along(x, axis, by):
    length = lax.axis_size(axis)
    return lax.ppermute(x, axis, [(i, (i + by) % length) for i in range(length)])


def finish(
    right_sum,
    left_sum,
    head_codes,
    tail_codes,
    mask_rows,
    pair_rows,
    split_weight,
    pair_weight,
    span_blocks,
    partition,
    owner_factor,
):
    cycles, tile_size = head_codes.shape
    repeat = tile_size // mask_rows.shape[1]
    allowed = jnp.repeat(
        jnp.repeat(mask_rows.astype(jnp.float32), repeat, axis=0), repeat, axis=1
    ).reshape(cycles, tile_size, tile_size)
    letters = jnp.arange(4, dtype=jnp.int32)
    head_hot = (head_codes[:, :, None] == letters[None, None, :]).astype(jnp.float32)
    tail_hot = (tail_codes[:, :, None] == letters[None, None, :]).astype(jnp.float32)
    head_weight = jnp.einsum("mak,k->ma", head_hot, split_weight, precision=precise)
    tail_weight = jnp.einsum("mak,k->ma", tail_hot, split_weight, precision=precise)
    outside_diag = (
        owner_factor
        * allowed
        * (right_sum * tail_weight[:, None, :] + head_weight[:, :, None] * left_sum)
        / tile_size
    )
    pair_table = jnp.einsum("mak,kl,mbl->mab", head_hot, pair_weight, tail_hot, precision=precise)
    positions = jnp.arange(tile_size, dtype=jnp.float32)
    span_nt = (
        tile_size * span_blocks[0].astype(jnp.float32) + positions[None, :] - positions[:, None]
    )
    penalty = jnp.sqrt(64.0 * tile_size / span_nt)
    pair_prob = (
        pair_rows.reshape(cycles, tile_size, tile_size)
        * outside_diag
        * pair_table
        * penalty[None, :, :]
        / partition[0]
    )
    return (
        outside_diag.reshape(cycles * tile_size, tile_size),
        pair_prob.reshape(cycles * tile_size, tile_size),
    )


def as_tiles(array):
    return array.reshape(-1, array.shape[1], array.shape[1])


def move_later(stack):
    return jnp.concatenate([jnp.zeros_like(stack), stack[:-1]], axis=0)


def per_device(
    outside,
    inside_head,
    inside_tail,
    inside_pair,
    seq_head,
    seq_tail,
    pair_mask,
    split_weight,
    pair_weight,
    span_blocks,
    partition,
):
    row_count = lax.axis_size("row")
    row_id = lax.axis_index("row")
    col_id = lax.axis_index("col")
    out_tiles = as_tiles(outside)
    right_part = jnp.einsum(
        "mac,mbc->mab", out_tiles, as_tiles(inside_tail), preferred_element_type=jnp.float32
    )
    window = passed_along(right_part, "col", -1)
    for level in range(row_count.bit_length() - 1):
        window = window + passed_along(window, "col", -(1 << level))
    reach = (col_id - row_id) % row_count
    reach = jnp.where(reach == 0, row_count, reach)
    left_part = jnp.einsum(
        "mca,mcb->mab", as_tiles(inside_head), out_tiles, preferred_element_type=jnp.float32
    )
    left_part = jnp.where(col_id < reach, move_later(left_part), left_part)
    left_sum = lax.psum(left_part, "row")
    owner_factor = (row_id == col_id % row_count).astype(jnp.float32)
    return finish(
        window,
        left_sum,
        seq_head,
        seq_tail,
        pair_mask,
        inside_pair,
        split_weight,
        pair_weight,
        span_blocks,
        partition,
        owner_factor,
    )


def solution(mesh):
    placed = (
        P("row", "col"),
        P("row", "col"),
        P("row", "col"),
        P(None, "col"),
        P(None, "col"),
        P(None, "col"),
        P(None, "col"),
        P(),
        P(),
        P(),
        P(),
    )
    return jax.shard_map(
        per_device,
        mesh=mesh,
        in_specs=placed,
        out_specs=(P("row", "col"), P("row", "col")),
        check_vma=False,
    )
```

profile of v0, /device:TPU:0, one launch (start us, length us, event | category | flops | bytes accessed | tf_op | source)
XLA Modules:
  0.0 118.1 jit_solution(13893284041892178920)
XLA Ops:
  7.2 0.0 copy-start
  7.2 0.0 all-reduce.2.cloned.1.call-start
  7.2 1.0 copy-done
  8.2 1.5 %convolution_bitcast_fusion.1 = f32[1,512,512]{2,1,0:T(8,128)S(1)} fusion(bf16[512,512]{1,0:T(8,128)(2,1)S(1)} %copy-done, bf16[512,512]{1,0:T(8,128)(2,1)} %param.13), kind=kOutput, calls=%fused_computation.3 | convolution fusion | flops 268435456 | bytes 2097152 | tf_op jit(solution)/shard_map/mac,mbc->mab/dot_general | solution.py:87
  9.7 6.1 %collective-permute-start = (f32[1,512,512]{2,1,0:T(8,128)S(1)}, f32[1,512,512]{2,1,0:T(8,128)S(1)}, u32[]{:S(2)}, u32[]{:S(2)}) collective-permute-start(f32[1,512,512]{2,1,0:T(8,128)S(1)} %convolution_bitcast_fusion.1), channel_id=1, source_target_pairs={{0,7},{1,0},{2,1},{3,2},{4,3},{5,4},{6,5},{7,6},{8,15},{9,8},{10,9... | collective-permute-start | bytes 3145736 | tf_op jit(solution)/shard_map/ppermute | solution.py:11
  15.8 22.4 %collective-permute-done = f32[1,512,512]{2,1,0:T(8,128)S(1)} collective-permute-done((f32[1,512,512]{2,1,0:T(8,128)S(1)}, f32[1,512,512]{2,1,0:T(8,128)S(1)}, u32[]{:S(2)}, u32[]{:S(2)}) %collective-permute-start) | collective-permute-done | bytes 1048608 | tf_op jit(solution)/shard_map/ppermute | solution.py:11
  38.2 5.2 %collective-permute-start.1 = (f32[1,512,512]{2,1,0:T(8,128)S(1)}, f32[1,512,512]{2,1,0:T(8,128)}, u32[]{:S(2)}, u32[]{:S(2)}) collective-permute-start(f32[1,512,512]{2,1,0:T(8,128)S(1)} %collective-permute-done), channel_id=1, source_target_pairs={{0,7},{1,0},{2,1},{3,2},{4,3},{5,4},{6,5},{7,6},{8,15},{9,8},{10,9... | collective-permute-start | bytes 3145736 | tf_op jit(solution)/shard_map/ppermute | solution.py:11
  43.4 21.6 %collective-permute-done.1 = f32[1,512,512]{2,1,0:T(8,128)} collective-permute-done((f32[1,512,512]{2,1,0:T(8,128)S(1)}, f32[1,512,512]{2,1,0:T(8,128)}, u32[]{:S(2)}, u32[]{:S(2)}) %collective-permute-start.1) | collective-permute-done | bytes 1048608 | tf_op jit(solution)/shard_map/ppermute | solution.py:11
  64.9 1.4 %add.30 = f32[1,512,512]{2,1,0:T(8,128)S(1)} add(f32[1,512,512]{2,1,0:T(8,128)S(1)} %collective-permute-done, f32[1,512,512]{2,1,0:T(8,128)} %collective-permute-done.1) | non-fusion elementwise | flops 262144 | bytes 3145728 | tf_op jit(solution)/shard_map/add | solution.py:92
  66.4 1.5 %collective-permute-start.2 = (f32[1,512,512]{2,1,0:T(8,128)S(1)}, f32[1,512,512]{2,1,0:T(8,128)}, u32[]{:S(2)}, u32[]{:S(2)}) collective-permute-start(f32[1,512,512]{2,1,0:T(8,128)S(1)} %add.30), channel_id=1, source_target_pairs={{0,6},{1,7},{2,0},{3,1},{4,2},{5,3},{6,4},{7,5},{8,14},{9,15},{10,... | collective-permute-start | bytes 3145736 | tf_op jit(solution)/shard_map/ppermute | solution.py:11
  67.8 0.0 copy-done.6
  67.8 1.4 %fusion = f32[1,512,512]{2,1,0:T(8,128)} fusion(bf16[512,512]{1,0:T(8,128)(2,1)S(1)} %copy-done.6, bf16[512,512]{1,0:T(8,128)(2,1)S(1)} %copy-done, pred[]{:T(512)S(6)} %lt.15), kind=kOutput, calls=%fused_computation.1 | convolution fusion | flops 268697600 | bytes 2097153 | tf_op jit(solution)/shard_map/mca,mcb->mab/dot_general | solution.py:95
  69.3 0.0 all-reduce.2.cloned.1.call-update
  69.3 0.0 copy-start.4
  69.3 0.7 copy-done.4
  70.0 0.6 broadcast_in_dim.7
  70.6 1.4 %mul.59 = f32[1,512,512]{2,1,0:T(8,128)} reshape(f32[512,4,128]{2,1,0:T(4,128)S(1)} %broadcast_in_dim.7) | data formatting | bytes 2097152 | tf_op jit(solution)/shard_map/mul | solution.py:38
  73.3 0.0 copy-start.7
  73.3 0.0 copy-start.8
  73.3 0.7 copy-done.7
  74.0 0.0 copy-done.8
  74.0 0.3 fusion.7
  74.3 0.7 copy-done.2
  75.0 0.3 fusion.6
  75.3 0.4 copy-done.3
  75.7 0.3 fusion.5
  76.0 30.8 %all-reduce.2.cloned.1.call-done = f32[1,512,512]{2,1,0:T(8,128)} async-done(((f32[1,512,512]{2,1,0:T(8,128)}), f32[1,512,512]{2,1,0:T(8,128)}) %all-reduce.2.cloned.1.call-update) | async-done | bytes 1048592 | tf_op jit(solution)/shard_map/psum | solution.py:99
  106.9 0.0 collective-permute-done.2
  106.9 2.2 %multiply_multiply_fusion = f32[1,512,512]{2,1,0:T(8,128)S(1)} fusion(f32[1,512,512]{2,1,0:T(8,128)} %mul.59, f32[1,512,512]{2,1,0:T(8,128)} %all-reduce.2.cloned.1.call-done, f32[1,512,512]{2,1,0:T(8,128)S(1)} %add.30, f32[1,512,512]{2,1,0:T(8,128)} %collective-permute-done.2, f32[512]{0:T(512)S(1)} %bitcast.46, f32[512]{0:T(512)S(1)} %bitcast.45), kind=kLoop, calls=%fused_computation.9 | loop fusion | flops 1572864 | bytes 5246976 | tf_op jit(solution)/shard_map/div | solution.py:38
  109.1 0.0 copy-start.1
  109.1 2.2 %fusion.4 = f32[512,512]{1,0:T(8,128)} fusion(f32[512,4]{1,0:T(8,128)S(1)} %fusion.5, f32[1,512,512]{2,1,0:T(8,128)S(1)} %multiply_multiply_fusion, f32[512,512]{1,0:T(8,128)S(1)} %copy-done.5, f32[]{:T(128)} %bitcast.40, f32[512]{0:T(512)S(1)} %iota_add_fusion, s32[512]{0:T(512)S(1)} %bitcast.48), kind=kOutput, calls=%fused_computation.7 | convolution fusion | flops 14157824 | bytes 3158020 | tf_op jit(solution)/shard_map/mak,kl,mbl->mab/dot_general | solution.py:43
  111.3 0.0 copy-done.1
  (8 shorter events, 0.1 us)
Async XLA Ops:
  7.2 1.0 copy-start
  7.2 99.7 %all-reduce.2.cloned.1.call-start = ((), (), s32[]{:S(2)}) async-start(), calls=%async_computation | async-start | bytes 2097152 | tf_op jit(solution)/shard_map/psum | solution.py:99
  9.7 28.5 %collective-permute-start = (f32[1,512,512]{2,1,0:T(8,128)S(1)}, f32[1,512,512]{2,1,0:T(8,128)S(1)}, u32[]{:S(2)}, u32[]{:S(2)}) collective-permute-start(f32[1,512,512]{2,1,0:T(8,128)S(1)} %convolution_bitcast_fusion.1), channel_id=1, source_target_pairs={{0,7},{1,0},{2,1},{3,2},{4,3},{5,4},{6,5},{7,6},{8,15},{9,8},{10,9... | collective-permute-start | bytes 3145736 | tf_op jit(solution)/shard_map/ppermute | solution.py:11
  38.2 26.7 %collective-permute-start.1 = (f32[1,512,512]{2,1,0:T(8,128)S(1)}, f32[1,512,512]{2,1,0:T(8,128)}, u32[]{:S(2)}, u32[]{:S(2)}) collective-permute-start(f32[1,512,512]{2,1,0:T(8,128)S(1)} %collective-permute-done), channel_id=1, source_target_pairs={{0,7},{1,0},{2,1},{3,2},{4,3},{5,4},{6,5},{7,6},{8,15},{9,8},{10,9... | collective-permute-start | bytes 3145736 | tf_op jit(solution)/shard_map/ppermute | solution.py:11
  43.4 24.5 %copy-start.6 = (bf16[512,512]{1,0:T(8,128)(2,1)S(1)}, bf16[512,512]{1,0:T(8,128)(2,1)}, u32[]{:S(2)}) copy-start(bf16[512,512]{1,0:T(8,128)(2,1)} %param.12) | copy-start | bytes 1572868
  66.4 40.5 %collective-permute-start.2 = (f32[1,512,512]{2,1,0:T(8,128)S(1)}, f32[1,512,512]{2,1,0:T(8,128)}, u32[]{:S(2)}, u32[]{:S(2)}) collective-permute-start(f32[1,512,512]{2,1,0:T(8,128)S(1)} %add.30), channel_id=1, source_target_pairs={{0,6},{1,7},{2,0},{3,1},{4,2},{5,3},{6,4},{7,5},{8,14},{9,15},{10,... | collective-permute-start | bytes 3145736 | tf_op jit(solution)/shard_map/ppermute | solution.py:11
  69.3 0.7 copy-start.4
  73.3 0.7 copy-start.7
  73.3 0.7 copy-start.8
  74.3 0.7 copy-start.2
  75.0 0.7 copy-start.3
  106.9 2.2 %copy-start.5 = (f32[512,512]{1,0:T(8,128)S(1)}, f32[512,512]{1,0:T(8,128)}, u32[]{:S(2)}) copy-start(f32[512,512]{1,0:T(8,128)} %param.14) | copy-start | bytes 3145732
  109.1 2.2 %copy-start.1 = (f32[1,512,512]{2,1,0:T(8,128)}, f32[1,512,512]{2,1,0:T(8,128)S(1)}, u32[]{:S(2)}) copy-start(f32[1,512,512]{2,1,0:T(8,128)S(1)} %multiply_multiply_fusion) | copy-start | bytes 3145732
Sparse Core Ops, SparseCore 0:
  69.4 37.4 all-reduce.1
where the time goes:
time: 118 us
  waiting for transfers between devices  74.8 us (63%)
  between operations  15.4 us (13%)
  starting transfers between devices  12.7 us (11%)
  matrix products  6.02 us (5%)
  local copies, waits for them, and re-layouts  5.42 us (5%)
  other arithmetic  3.66 us (3%)
    ppermute x3, waiting for transfers between devices, passed_along(): lax.ppermute(x, axis, [(i, (i + by) % length) for i in range(length)])  44 us
    psum x1, waiting for transfers between devices, per_device(): left_sum = lax.psum(left_part, 'row')  30.8 us
    ppermute x3, starting transfers between devices, passed_along(): lax.ppermute(x, axis, [(i, (i + by) % length) for i in range(length)])  12.7 us
    unnamed x18, local copies, waits for them, and re-layouts  3.4 us
    dot_general x2, matrix products, finish(): jnp.einsum('mak,kl,mbl->mab', head_hot, pair_weight, tail_hot, precision=...  2.47 us
  transfers between devices with their start and end apart: 4, of which 3 were waited for; matrix products, arithmetic and copies ran while one was open for 4% of the time, Pallas kernels for 0%

commit v1 on v0

--- a/solution.py
+++ b/solution.py
@@ -2,6 +2,7 @@
 import jax.numpy as jnp
 from jax import lax
 from jax.sharding import PartitionSpec as P
+from jax.lax import all_gather
 
 precise = lax.Precision.HIGHEST
 
@@ -96,7 +97,7 @@
         "mca,mcb->mab", as_tiles(inside_head), out_tiles, preferred_element_type=jnp.float32
     )
     left_part = jnp.where(col_id < reach, move_later(left_part), left_part)
-    left_sum = lax.psum(left_part, "row")
+    left_sum = all_gather(left_part, "row").sum(axis=0)
     owner_factor = (row_id == col_id % row_count).astype(jnp.float32)
     return finish(
         window,

time: 118 us -> 103 us (0.87); the launches traced: 118 us -> 102 us
  waiting for transfers between devices: 74.8 us -> 57.8 us
  local copies, waits for them, and re-layouts: 5.42 us -> 3.03 us
  other arithmetic: 3.66 us -> 5.78 us
    psum x1 -> x0, waiting for transfers between devices: 30.8 us -> none  [per_device(): left_sum = lax.psum(left_part, 'row')]
    ppermute x3, waiting for transfers between devices: 44 us -> 57.7 us  [passed_along(): lax.ppermute(x, axis, [(i, (i + by) % length) for i in range(length)])]
    reduce_sum x0 -> x1, other arithmetic: none -> 3.76 us  [per_device(): left_sum = all_gather(left_part, 'row').sum(axis=0)]
    unnamed x18, local copies, waits for them, and re-layouts: 3.4 us -> 1.01 us
    add x1, other arithmetic: 1.43 us -> 0.21 us  [per_device(): window = window + passed_along(window, 'col', -(1 << level))]
  transfers between devices with their start and end apart: 4 -> 4, of which waited for: 3 -> 3; matrix products, arithmetic and copies ran while one was open for 4% -> 8% of each run, Pallas kernels for 0% -> 0%
where the time goes in v1:
time: 103 us; the launch traced here: 102 us
  waiting for transfers between devices  57.8 us (56%)
  between operations  15.6 us (15%)
  starting transfers between devices  12.6 us (12%)
  matrix products  7.14 us (7%)
  other arithmetic  5.78 us (6%)
  local copies, waits for them, and re-layouts  3.03 us (3%)
    ppermute x3, waiting for transfers between devices, passed_along(): lax.ppermute(x, axis, [(i, (i + by) % length) for i in range(length)])  57.7 us
    ppermute x3, starting transfers between devices, passed_along(): lax.ppermute(x, axis, [(i, (i + by) % length) for i in range(length)])  12.6 us
    reduce_sum x1, other arithmetic, per_device(): left_sum = all_gather(left_part, 'row').sum(axis=0)  3.76 us
    dot_general x2, matrix products, finish(): jnp.einsum('mak,kl,mbl->mab', head_hot, pair_weight, tail_hot, precision=...  2.49 us
    dot_general x1, matrix products, per_device(): jnp.einsum('mca,mcb->mab', as_tiles(inside_head), out_tiles, preferred_el...  2.49 us
  transfers between devices with their start and end apart: 4, of which 3 were waited for; matrix products, arithmetic and copies ran while one was open for 8% of the time, Pallas kernels for 0%

profile of v1, /device:TPU:0, one launch (start us, length us, event | category | flops | bytes accessed | tf_op | source)
XLA Modules:
  0.0 101.9 jit_solution(4818374428400599966)
XLA Ops:
  7.2 0.0 copy-start
  7.2 0.0 all-gather.3.cloned.1.call-start
  7.3 1.0 copy-done
  8.2 2.5 %convolution_select_fusion = f32[512,512]{1,0:T(8,128)} fusion(bf16[512,512]{1,0:T(8,128)(2,1)} %param.12, bf16[512,512]{1,0:T(8,128)(2,1)S(1)} %copy-done, pred[]{:T(512)S(6)} %lt.15), kind=kOutput, calls=%fused_computation | convolution fusion | flops 268697600 | bytes 2097153 | tf_op jit(solution)/shard_map/mca,mcb->mab/dot_general | solution.py:96
  10.7 0.0 all-gather.3.cloned.1.call-update
  10.7 0.0 copy-start.7
  10.7 0.0 copy-start.8
  10.8 0.0 copy-start.3
  10.8 0.0 copy-start.4
  10.8 1.5 %convolution_bitcast_fusion.1 = f32[1,512,512]{2,1,0:T(8,128)S(1)} fusion(bf16[512,512]{1,0:T(8,128)(2,1)S(1)} %copy-done, bf16[512,512]{1,0:T(8,128)(2,1)} %param.13), kind=kOutput, calls=%fused_computation.2 | convolution fusion | flops 268435456 | bytes 2097152 | tf_op jit(solution)/shard_map/mac,mbc->mab/dot_general | solution.py:88
  12.3 6.1 %collective-permute-start = (f32[1,512,512]{2,1,0:T(8,128)S(1)}, f32[1,512,512]{2,1,0:T(8,128)S(1)}, u32[]{:S(2)}, u32[]{:S(2)}) collective-permute-start(f32[1,512,512]{2,1,0:T(8,128)S(1)} %convolution_bitcast_fusion.1), channel_id=1, source_target_pairs={{0,7},{1,0},{2,1},{3,2},{4,3},{5,4},{6,5},{7,6},{8,15},{9,8},{10,9... | collective-permute-start | bytes 3145736 | tf_op jit(solution)/shard_map/ppermute | solution.py:12
  18.4 22.4 %collective-permute-done = f32[1,512,512]{2,1,0:T(8,128)S(1)} collective-permute-done((f32[1,512,512]{2,1,0:T(8,128)S(1)}, f32[1,512,512]{2,1,0:T(8,128)S(1)}, u32[]{:S(2)}, u32[]{:S(2)}) %collective-permute-start) | collective-permute-done | bytes 1048608 | tf_op jit(solution)/shard_map/ppermute | solution.py:12
  40.8 5.2 %collective-permute-start.1 = (f32[1,512,512]{2,1,0:T(8,128)S(1)}, f32[1,512,512]{2,1,0:T(8,128)S(1)}, u32[]{:S(2)}, u32[]{:S(2)}) collective-permute-start(f32[1,512,512]{2,1,0:T(8,128)S(1)} %collective-permute-done), channel_id=1, source_target_pairs={{0,7},{1,0},{2,1},{3,2},{4,3},{5,4},{6,5},{7,6},{8,15},{9,8},{10,9... | collective-permute-start | bytes 3145736 | tf_op jit(solution)/shard_map/ppermute | solution.py:12
  46.0 21.6 %collective-permute-done.1 = f32[1,512,512]{2,1,0:T(8,128)S(1)} collective-permute-done((f32[1,512,512]{2,1,0:T(8,128)S(1)}, f32[1,512,512]{2,1,0:T(8,128)S(1)}, u32[]{:S(2)}, u32[]{:S(2)}) %collective-permute-start.1) | collective-permute-done | bytes 1048608 | tf_op jit(solution)/shard_map/ppermute | solution.py:12
  67.5 0.2 add.28
  67.7 1.4 %collective-permute-start.2 = (f32[1,512,512]{2,1,0:T(8,128)S(1)}, f32[1,512,512]{2,1,0:T(8,128)}, u32[]{:S(2)}, u32[]{:S(2)}) collective-permute-start(f32[1,512,512]{2,1,0:T(8,128)S(1)} %add.28), channel_id=1, source_target_pairs={{0,6},{1,7},{2,0},{3,1},{4,2},{5,3},{6,4},{7,5},{8,14},{9,15},{10,... | collective-permute-start | bytes 3145736 | tf_op jit(solution)/shard_map/ppermute | solution.py:12
  69.1 0.0 copy-done.5
  69.1 0.6 broadcast_in_dim.7
  69.7 1.4 %mul.67 = f32[1,512,512]{2,1,0:T(8,128)} reshape(f32[512,4,128]{2,1,0:T(4,128)S(1)} %broadcast_in_dim.7) | data formatting | bytes 2097152 | tf_op jit(solution)/shard_map/mul | solution.py:39
  72.5 0.0 copy-done.7
  72.5 0.0 copy-done.8
  72.5 0.3 fusion.9
  72.8 0.0 copy-done.3
  72.8 0.3 fusion.8
  73.2 0.0 copy-done.4
  73.2 0.3 fusion.7
  73.5 0.0 all-gather.3.cloned.1.call-done
  73.6 3.8 %reduce.1 = f32[512,512]{1,0:T(8,128)} reduce(f32[4,512,512]{2,1,0:T(8,128)} %bitcast.48, f32[]{:T(128)} %constant.33.clone.1), dimensions={0}, to_apply=%region_0.1 | reduce | flops 786432 | bytes 5242884 | tf_op jit(solution)/shard_map/reduce_sum | solution.py:100
  77.3 13.8 %collective-permute-done.2 = f32[1,512,512]{2,1,0:T(8,128)} collective-permute-done((f32[1,512,512]{2,1,0:T(8,128)S(1)}, f32[1,512,512]{2,1,0:T(8,128)}, u32[]{:S(2)}, u32[]{:S(2)}) %collective-permute-start.2) | collective-permute-done | bytes 1048608 | tf_op jit(solution)/shard_map/ppermute | solution.py:12
  91.1 1.8 %fusion.6 = f32[1,512,512]{2,1,0:T(8,128)S(1)} fusion(f32[1,512,512]{2,1,0:T(8,128)S(1)} %copy-done.1, f32[512,512]{1,0:T(8,128)} %reduce.1, f32[1,512,512]{2,1,0:T(8,128)S(1)} %add.28, f32[1,512,512]{2,1,0:T(8,128)} %collective-permute-done.2, f32[512]{0:T(512)S(1)} %bitcast.54, f32[512]{0:T(512)S(1)} %bitcast.53), kind=kLoop, calls=%fused_computation.11 | loop fusion | flops 1572864 | bytes 5246976 | tf_op jit(solution)/shard_map/div | solution.py:39
  92.9 0.0 copy-start.2
  92.9 2.2 %fusion.3 = f32[512,512]{1,0:T(8,128)} fusion(f32[512,4]{1,0:T(8,128)S(1)} %fusion.7, f32[1,512,512]{2,1,0:T(8,128)S(1)} %fusion.6, f32[512,512]{1,0:T(8,128)S(1)} %copy-done.6, f32[]{:T(128)} %bitcast.47, f32[512]{0:T(512)S(1)} %iota_add_fusion, s32[512]{0:T(512)S(1)} %bitcast.56), kind=kOutput, calls=%fused_computation.6 | convolution fusion | flops 14157824 | bytes 3158020 | tf_op jit(solution)/shard_map/mak,kl,mbl->mab/dot_general | solution.py:44
  (9 shorter events, 0.0 us)
Async XLA Ops:
  7.2 1.0 %copy-start = (bf16[512,512]{1,0:T(8,128)(2,1)S(1)}, bf16[512,512]{1,0:T(8,128)(2,1)}, u32[]{:S(2)}) copy-start(bf16[512,512]{1,0:T(8,128)(2,1)} %param.11) | copy-start | bytes 1572868
  7.2 66.4 %all-gather.3.cloned.1.call-start = ((), (), s32[]{:S(2)}) async-start(), calls=%async_computation | async-start | bytes 5242880 | tf_op jit(solution)/shard_map/all_gather | solution.py:100
  8.2 60.9 %copy-start.5 = (s32[4,4]{1,0:T(4,128)S(1)}, s32[4,4]{1,0:T(4,128)}, u32[]{:S(2)}) copy-start(s32[4,4]{1,0:T(4,128)} %param.17) | copy-start | bytes 196
  10.7 61.8 %copy-start.7 = (s32[1,512]{1,0:T(1,128)S(1)}, s32[1,512]{1,0:T(1,128)}, u32[]{:S(2)}) copy-start(s32[1,512]{1,0:T(1,128)} %param.16) | copy-start | bytes 6148
  10.7 61.8 %copy-start.8 = (f32[4]{0:T(128)S(1)}, f32[4]{0:T(128)}, u32[]{:S(2)}) copy-start(f32[4]{0:T(128)} %param.18) | copy-start | bytes 52
  10.8 62.1 %copy-start.3 = (s32[1,512]{1,0:T(1,128)S(1)}, s32[1,512]{1,0:T(1,128)}, u32[]{:S(2)}) copy-start(s32[1,512]{1,0:T(1,128)} %param.15) | copy-start | bytes 6148
  10.8 62.4 %copy-start.4 = (f32[4,4]{1,0:T(4,128)S(1)}, f32[4,4]{1,0:T(4,128)}, u32[]{:S(2)}) copy-start(f32[4,4]{1,0:T(4,128)} %param.19) | copy-start | bytes 196
  12.3 28.5 %collective-permute-start = (f32[1,512,512]{2,1,0:T(8,128)S(1)}, f32[1,512,512]{2,1,0:T(8,128)S(1)}, u32[]{:S(2)}, u32[]{:S(2)}) collective-permute-start(f32[1,512,512]{2,1,0:T(8,128)S(1)} %convolution_bitcast_fusion.1), channel_id=1, source_target_pairs={{0,7},{1,0},{2,1},{3,2},{4,3},{5,4},{6,5},{7,6},{8,15},{9,8},{10,9... | collective-permute-start | bytes 3145736 | tf_op jit(solution)/shard_map/ppermute | solution.py:12
  40.8 26.7 %collective-permute-start.1 = (f32[1,512,512]{2,1,0:T(8,128)S(1)}, f32[1,512,512]{2,1,0:T(8,128)S(1)}, u32[]{:S(2)}, u32[]{:S(2)}) collective-permute-start(f32[1,512,512]{2,1,0:T(8,128)S(1)} %collective-permute-done), channel_id=1, source_target_pairs={{0,7},{1,0},{2,1},{3,2},{4,3},{5,4},{6,5},{7,6},{8,15},{9,8},{10,9... | collective-permute-start | bytes 3145736 | tf_op jit(solution)/shard_map/ppermute | solution.py:12
  67.7 23.3 %collective-permute-start.2 = (f32[1,512,512]{2,1,0:T(8,128)S(1)}, f32[1,512,512]{2,1,0:T(8,128)}, u32[]{:S(2)}, u32[]{:S(2)}) collective-permute-start(f32[1,512,512]{2,1,0:T(8,128)S(1)} %add.28), channel_id=1, source_target_pairs={{0,6},{1,7},{2,0},{3,1},{4,2},{5,3},{6,4},{7,5},{8,14},{9,15},{10,... | collective-permute-start | bytes 3145736 | tf_op jit(solution)/shard_map/ppermute | solution.py:12
  71.1 20.0 %copy-start.1 = (f32[1,512,512]{2,1,0:T(8,128)S(1)}, f32[1,512,512]{2,1,0:T(8,128)}, u32[]{:S(2)}) copy-start(f32[1,512,512]{2,1,0:T(8,128)} %mul.67) | copy-start | bytes 3145732
  77.3 15.6 %copy-start.6 = (f32[512,512]{1,0:T(8,128)S(1)}, f32[512,512]{1,0:T(8,128)}, u32[]{:S(2)}) copy-start(f32[512,512]{1,0:T(8,128)} %param.14) | copy-start | bytes 3145732
  92.9 2.2 %copy-start.2 = (f32[1,512,512]{2,1,0:T(8,128)}, f32[1,512,512]{2,1,0:T(8,128)S(1)}, u32[]{:S(2)}) copy-start(f32[1,512,512]{2,1,0:T(8,128)S(1)} %fusion.6) | copy-start | bytes 3145732
Sparse Core Ops, SparseCore 0:
  10.8 37.1 all-gather.2
